TPU v7x, 128 devices: a whole 4x4x4 slice. The times are simulated.
128 devices in a mesh: req: 16 (over z, y), kv: 8 (over x, core).
Axes of the slice: x: 4, y: 4, z: 4, core: 2. Of those that a mesh axis runs over, the one named last changes fastest.
Arguments:
- hidden_in: bfloat16 [16384, 2048], P(('req', 'kv')), may hold values from -6 to 6
- slot_tokens: int32 [16384], replicated, may hold values from 0 to 16383, as said below
- cache_len: int32 [128], P('req'), may hold values from 1 to 2048, 65536 in all
- prefill_start: int32 [16], P('req'), may hold values from 0 to 2048
- key_cache: bfloat16 [128, 2048, 1024], P('req', None, 'kv')
- value_cache: bfloat16 [128, 2048, 1024], P('req', None, 'kv'), may hold values from -18 to 18
- key_prefix: bfloat16 [16, 2048, 1024], P('req', None, 'kv')
- value_prefix: bfloat16 [16, 2048, 1024], P('req', None, 'kv'), may hold values from -18 to 18
- attn_gain: float32 [2048], replicated, may hold values from 0.25 to 1.75
- q_proj: bfloat16 [2048, 2048], P(None, 'kv'), may hold values from -0.125 to 0.125
- k_proj: bfloat16 [2048, 1024], P(None, 'kv'), may hold values from -0.125 to 0.125
- v_proj: bfloat16 [2048, 1024], P(None, 'kv'), may hold values from -0.125 to 0.125
- q_gain: float32 [128], replicated, may hold values from 0.25 to 1.75
- k_gain: float32 [128], replicated, may hold values from 0.25 to 1.75
- o_proj: bfloat16 [2048, 2048], P('kv'), may hold values from -0.125 to 0.125
- ffn_gain: float32 [2048], replicated, may hold values from 0.25 to 1.75
- w_gate: bfloat16 [2048, 6144], P(None, 'req'), may hold values from -0.125 to 0.125
- w_up: bfloat16 [2048, 6144], P(None, 'req'), may hold values from -0.125 to 0.125
- w_down: bfloat16 [6144, 2048], P('req'), may hold values from -0.078125 to 0.078125
- final_gain: float32 [2048], replicated, may hold values from 0.25 to 1.75
- lm_head: bfloat16 [2048, 151936], P(None, ('req', 'kv')), may hold values from -0.375 to 0.375
Outputs:
- layer_out: bfloat16 [16384, 2048], P(('req', 'kv'))
- max_logit: float32 [144], replicated
Inputs may be any that keep to these rules, and one draw needn't show every extreme that they name: slot_tokens is a permutation of the batch's tokens; each device's 128 consecutive slots take exactly 1 token from each device's 128 consecutive batch tokens.
All inputs are finite; a program needn't handle non-finite values. No bound on the sum of `cache_len` on one device may be relied on, other than what follows from the above.
Results may differ from a plain program's by a relative error of at most 0.0085.
The roundings to bfloat16 on the way count: a program that leaves them out, or rounds other values in their place, can miss the bound.
Values may be sent and summed in bfloat16 or wider, within the bound.
A program may use at most 128 MiB of HBM per device.

v0:
```python
import jax
import jax.numpy as jnp
from jax import lax
from jax.sharding import PartitionSpec as P

EPS = 1e-06
NEG = -1e30


def spread(value, axis, root):
    mine = lax.axis_index(axis) == root
    return lax.psum(jnp.where(mine, value, jnp.zeros_like(value)), axis)


def norm_rows(values, gain_vec):
    wide = values.astype(jnp.float32)
    return wide * lax.rsqrt(jnp.mean(wide * wide, axis=-1, keepdims=True) + EPS) * gain_vec


def rotate(values, places):
    half_dim = values.shape[-1] // 2
    freqs = 1000000.0 ** (-(jnp.arange(half_dim, dtype=jnp.float32) * 2.0 / values.shape[-1]))
    angles = places[:, None] * freqs[None, :]
    cosine = jnp.cos(angles)[:, None, :]
    sine = jnp.sin(angles)[:, None, :]
    first_half = values[..., :half_dim]
    second_half = values[..., half_dim:]
    return jnp.concatenate(
        [first_half * cosine - second_half * sine, second_half * cosine + first_half * sine],
        axis=-1,
    )


def prefill_full(q_heads, key_old, value_old, key_new, value_new, start_at):
    old_len = key_old.shape[0]
    fresh_rows = q_heads.shape[0]
    factor = q_heads.shape[-1] ** (-0.5)
    all_keys = jnp.concatenate([key_old, key_new], axis=0)
    all_values = jnp.concatenate([value_old, value_new], axis=0)
    scores = (
        jnp.einsum("cgd,kd->gck", q_heads, all_keys, preferred_element_type=jnp.float32) * factor
    )
    key_index = jnp.arange(old_len + fresh_rows, dtype=jnp.int32)[None, :]
    row_index = jnp.arange(fresh_rows, dtype=jnp.int32)[:, None]
    allowed = jnp.where(key_index < old_len, key_index < start_at, key_index - old_len <= row_index)
    scores = jnp.where(allowed[None], scores, NEG)
    row_peak = jnp.max(scores, axis=-1, keepdims=True)
    expd = jnp.exp(scores - row_peak)
    weights = (expd / jnp.sum(expd, axis=-1, keepdims=True)).astype(jnp.bfloat16)
    return jnp.einsum(
        "gck,kd->cgd", weights, all_values, preferred_element_type=jnp.float32
    ).astype(jnp.bfloat16)


def decode_attend(q_heads, key_old, value_old, key_self, value_self, lengths):
    factor = q_heads.shape[-1] ** (-0.5)
    past = jnp.einsum("bgd,bld->bgl", q_heads, key_old, preferred_element_type=jnp.float32) * factor
    slot_index = jnp.arange(key_old.shape[1], dtype=jnp.int32)
    past = jnp.where(slot_index[None, None, :] < lengths[:, None, None], past, NEG)
    own_score = (
        jnp.einsum("bgd,bd->bg", q_heads, key_self, preferred_element_type=jnp.float32) * factor
    )
    row_peak = jnp.maximum(jnp.max(past, axis=-1), own_score)
    past_exp = jnp.exp(past - row_peak[..., None])
    own_exp = jnp.exp(own_score - row_peak)
    row_total = jnp.sum(past_exp, axis=-1) + own_exp
    past_w = (past_exp / row_total[..., None]).astype(jnp.bfloat16)
    own_w = (own_exp / row_total).astype(jnp.bfloat16)
    summed = jnp.einsum("bgl,bld->bgd", past_w, value_old, preferred_element_type=jnp.float32)
    summed = (
        summed + own_w.astype(jnp.float32)[..., None] * value_self.astype(jnp.float32)[:, None, :]
    )
    return summed.astype(jnp.bfloat16)


def regroup(rows_in):
    return lax.all_to_all(rows_in, ("req", "kv"), split_axis=0, concat_axis=0, tiled=True)


def shards(
    hidden_in,
    slot_tokens,
    cache_len,
    prefill_start,
    key_cache,
    value_cache,
    key_prefix,
    value_prefix,
    attn_gain,
    q_proj,
    k_proj,
    v_proj,
    q_gain,
    k_gain,
    o_proj,
    ffn_gain,
    w_gate,
    w_up,
    w_down,
    final_gain,
    lm_head,
):
    req_count = lax.axis_size("req")
    kv_count = lax.axis_size("kv")
    devices = req_count * kv_count
    rows_dev = hidden_in.shape[0]
    kv_index = lax.axis_index("kv")
    self_index = lax.axis_index("req") * kv_count + kv_index
    slot_table = slot_tokens.reshape(devices, rows_dev)
    from_self = slot_table // rows_dev == self_index
    send_rows = jnp.sum(jnp.where(from_self, slot_table - self_index * rows_dev, 0), axis=1)
    slot_place = lax.dynamic_index_in_dim(slot_table, self_index, 0, keepdims=False) // rows_dev
    arrived = regroup(hidden_in[send_rows])
    owner_rows = arrived[slot_place]
    rows_all = lax.all_gather(owner_rows, "kv", axis=0, tiled=True)
    normed = norm_rows(rows_all, attn_gain).astype(jnp.bfloat16)
    o_full = lax.all_gather(o_proj, "kv", axis=0, tiled=True)
    ff_dev = w_gate.shape[1]
    ff_piece = ff_dev // kv_count
    gate_w = lax.all_gather(
        lax.dynamic_slice_in_dim(w_gate, kv_index * ff_piece, ff_piece, axis=1),
        "req",
        axis=1,
        tiled=True,
    )
    up_w = lax.all_gather(
        lax.dynamic_slice_in_dim(w_up, kv_index * ff_piece, ff_piece, axis=1),
        "req",
        axis=1,
        tiled=True,
    )
    down_w = lax.all_gather(
        lax.dynamic_slice_in_dim(w_down, kv_index * ff_piece, ff_piece, axis=0),
        "req",
        axis=0,
        tiled=True,
    )
    q_cols = q_proj.shape[1]
    kv_cols = k_proj.shape[1]
    projected = jnp.concatenate(
        [
            jnp.dot(normed, q_proj, preferred_element_type=jnp.float32),
            jnp.dot(normed, k_proj, preferred_element_type=jnp.float32),
            jnp.dot(normed, v_proj, preferred_element_type=jnp.float32),
        ],
        axis=1,
    )
    tok_req = projected.shape[0]
    head_dim = q_gain.shape[0]
    dec_count = cache_len.shape[0]
    fresh_count = tok_req - dec_count
    q_raw = projected[:, :q_cols].reshape(tok_req, q_cols // head_dim, head_dim)
    k_raw = projected[:, q_cols : q_cols + kv_cols].reshape(tok_req, kv_cols // head_dim, head_dim)
    v_new = (
        projected[:, q_cols + kv_cols :]
        .astype(jnp.bfloat16)
        .reshape(tok_req, kv_cols // head_dim, head_dim)
    )
    places = jnp.concatenate(
        [prefill_start[0] + jnp.arange(fresh_count, dtype=jnp.int32), cache_len]
    ).astype(jnp.float32)
    queries = rotate(norm_rows(q_raw, q_gain), places).astype(jnp.bfloat16)
    keys_new = rotate(norm_rows(k_raw, k_gain), places).astype(jnp.bfloat16)
    pre_out = prefill_full(
        queries[:fresh_count],
        key_prefix[0, :, 0:head_dim],
        value_prefix[0, :, 0:head_dim],
        keys_new[:fresh_count, 0],
        v_new[:fresh_count, 0],
        prefill_start[0],
    )
    dec_out = decode_attend(
        queries[fresh_count:],
        key_cache,
        value_cache,
        keys_new[fresh_count:, 0],
        v_new[fresh_count:, 0],
        cache_len,
    )
    pieces = jnp.concatenate([pre_out, dec_out], axis=0)
    pieces, gate_w, up_w, down_w = lax.optimization_barrier((pieces, gate_w, up_w, down_w))
    attended = lax.all_gather(pieces.reshape(tok_req, q_cols), "kv", axis=1, tiled=True)
    resid = (
        rows_all.astype(jnp.float32) + jnp.dot(attended, o_full, preferred_element_type=jnp.float32)
    ).astype(jnp.bfloat16)
    ffn_in = norm_rows(resid, ffn_gain).astype(jnp.bfloat16)
    gate_part = jnp.dot(ffn_in, gate_w, preferred_element_type=jnp.float32)
    up_part = jnp.dot(ffn_in, up_w, preferred_element_type=jnp.float32)
    hidden_act = (jax.nn.silu(gate_part) * up_part).astype(jnp.bfloat16)
    down_part = jnp.dot(hidden_act, down_w, preferred_element_type=jnp.float32)
    ffn_part = lax.psum_scatter(down_part, "kv", scatter_dimension=0, tiled=True)
    mine = lax.dynamic_slice_in_dim(resid, kv_index * rows_dev, rows_dev, axis=0)
    out_rows = (mine.astype(jnp.float32) + ffn_part).astype(jnp.bfloat16)
    going_back = jnp.zeros_like(out_rows).at[slot_place].set(out_rows)
    returned = regroup(going_back)
    layer_out = jnp.zeros_like(hidden_in).at[send_rows].set(returned)
    tail_sum = lax.psum(down_part[fresh_count - 1 :], "kv")
    tail_out = (resid[fresh_count - 1 :].astype(jnp.float32) + tail_sum).astype(jnp.bfloat16)
    tail_rows = norm_rows(tail_out, final_gain).astype(jnp.bfloat16)
    local_peaks = jnp.max(
        jnp.dot(
            lax.all_gather(tail_rows, "req", axis=0, tiled=True),
            lm_head,
            preferred_element_type=jnp.float32,
        ),
        axis=1,
    )
    max_logit = lax.pmax(local_peaks, ("req", "kv"))
    return (layer_out, max_logit)


def solution(mesh):
    placed = (
        P(("req", "kv"), None),
        P(),
        P("req"),
        P("req"),
        P("req", None, "kv"),
        P("req", None, "kv"),
        P("req", None, "kv"),
        P("req", None, "kv"),
        P(),
        P(None, "kv"),
        P(None, "kv"),
        P(None, "kv"),
        P(),
        P(),
        P("kv", None),
        P(),
        P(None, "req"),
        P(None, "req"),
        P("req", None),
        P(),
        P(None, ("req", "kv")),
    )
    return jax.shard_map(
        shards, mesh=mesh, in_specs=placed, out_specs=(P(("req", "kv"), None), P()), check_vma=False
    )
```

profile of v0, /device:TPU:1, one launch (start us, length us, event | category | flops | bytes accessed | tf_op | source)
XLA Modules:
  0.0 573.7 jit_solution(5138658079195809557)
XLA Ops:
  8.3 2.6 gather_fusion
  13.5 11.5 %all-to-all-start = ((bf16[128,2,1024]{2,1,0:T(2,128)(2,1)}), bf16[128,2,1024]{2,1,0:T(2,128)(2,1)S(1)}, u32[]{:S(2)}, u32[]{:S(2)}) async-start(bf16[128,2,1024]{2,1,0:T(2,128)(2,1)} %reshape.450), calls=%async_computation | async-start | bytes 1048576 | tf_op jit(solution)/shard_map/all_to_all | solution.py:77
  25.8 13.0 %all-to-all-done = bf16[128,2,1024]{2,1,0:T(2,128)(2,1)S(1)} async-done(((bf16[128,2,1024]{2,1,0:T(2,128)(2,1)}), bf16[128,2,1024]{2,1,0:T(2,128)(2,1)S(1)}, u32[]{:S(2)}, u32[]{:S(2)}) %all-to-all-start) | async-done | bytes 524320 | tf_op jit(solution)/shard_map/all_to_all | solution.py:77
  39.5 1.7 gather_fusion.1
  44.9 1.6 constant_dynamic-slice_fusion
  48.5 1.9 multiply_cosine_fusion
  50.5 4.0 fusion.4
  54.5 15.7 %all-gather.19.cloned.1.call-done = bf16[1024,2048]{1,0:T(8,128)(2,1)} async-done(((bf16[128,2048]{1,0:T(8,128)(2,1)}), bf16[1024,2048]{1,0:T(8,128)(2,1)}) %all-gather.19.cloned.1.call-update) | async-done | bytes 4194320 | tf_op jit(solution)/shard_map/all_gather | solution.py:115
  70.1 3.2 fusion.10
  74.8 2.3 multiply_reduce_fusion
  77.1 1.6 copy.48
  78.7 3.7 multiply_reduce_fusion.1
  88.2 3.6 convolution_convert_fusion
  92.6 15.9 %fusion.78 = (f32[2,1016]{1,0:T(2,128)S(1)}, f32[2,1016,3064]{2,1,0:T(8,128)}) fusion(pred[1016,3064]{1,0:T(8,128)(4,1)} %fusion.4, bf16[1016,128]{1,0:T(8,128)(2,1)S(1)} %copy.47, bf16[2048,128]{1,0:T(8,128)(2,1)S(1)} %bitcast.93, bf16[1024,2,64]{2,0,1:T(8,128)(2,1)S(1)} %get-tuple-element.10, bf16[1024,2,64]{2,0,1:T(8,128)(2,1)S(1)} %get-tuple-element.11), kind=kOutput, calls=%fused_computation.144 | convolution fusion | flops 1621384704 | bytes 29334016 | tf_op jit(solution)/shard_map/sub | solution.py:48
  108.5 12.0 %fusion.18 = bf16[1016,2,128]{2,0,1:T(8,128)(2,1)S(1)} fusion(f32[2,1016,3064]{2,1,0:T(8,128)} %get-tuple-element.25, f32[2,1016]{1,0:T(2,128)S(1)} %get-tuple-element.24, bf16[1016,128]{1,0:T(8,128)(2,1)S(1)} %slice.54, bf16[2048,128]{1,0:T(8,128)(2,1)S(1)} %bitcast.94), kind=kOutput, calls=%fused_computation.32 | convolution fusion | flops 1608149248 | bytes 26216896 | tf_op jit(solution)/shard_map/gck,kd->cgd/dot_general | solution.py:50
  120.6 48.2 %all-gather.11.cloned.1.call-done = bf16[2048,768]{0,1:T(8,128)(2,1)} async-done(((bf16[2048,48]{0,1:T(8,128)(2,1)}), bf16[2048,768]{0,1:T(8,128)(2,1)}) %all-gather.11.cloned.1.call-update) | async-done | bytes 3145744 | tf_op jit(solution)/shard_map/all_gather | solution.py:126
  168.8 48.9 %all-gather.13.cloned.1.call-done = bf16[768,2048]{1,0:T(8,128)(2,1)} async-done(((bf16[48,2048]{1,0:T(8,128)(2,1)}), bf16[768,2048]{1,0:T(8,128)(2,1)}) %all-gather.13.cloned.1.call-update) | async-done | bytes 3145744 | tf_op jit(solution)/shard_map/all_gather | solution.py:132
  218.8 49.7 %all-gather.17.cloned.1.call-done = bf16[2048,2048]{1,0:T(8,128)(2,1)} async-done(((bf16[256,2048]{1,0:T(8,128)(2,1)}), bf16[2048,2048]{1,0:T(8,128)(2,1)}) %all-gather.17.cloned.1.call-update) | async-done | bytes 8388624 | tf_op jit(solution)/shard_map/all_gather | solution.py:117
  268.5 34.4 %all-gather.15.cloned.1.call-done = bf16[1024,2048]{0,1:T(8,128)(2,1)} async-done(((bf16[1024,256]{0,1:T(8,128)(2,1)}), bf16[1024,2048]{0,1:T(8,128)(2,1)}) %all-gather.15.cloned.1.call-update) | async-done | bytes 4194320 | tf_op jit(solution)/shard_map/all_gather | solution.py:182
  302.9 14.2 %fusion.7 = (f32[1024]{0:T(1024)S(1)}, bf16[1024,2048]{1,0:T(8,128)(2,1)S(1)}) fusion(bf16[1024,2048]{0,1:T(8,128)(2,1)} %all-gather.15.cloned.1.call-done, bf16[2048,2048]{1,0:T(8,128)(2,1)} %all-gather.17.cloned.1.call-done, bf16[1024,2048]{1,0:T(8,128)(2,1)} %all-gather.19.cloned.1.call-done), kind=kOutput, calls=%fused_computation.20 | convolution fusion | flops 8602516480 | bytes 20975616 | tf_op jit(solution)/shard_map/dot_general | solution.py:184
  317.1 1.9 copy-done.7
  319.0 7.1 %fusion.20 = f32[1024,768]{1,0:T(8,128)} fusion(bf16[2048,768]{0,1:T(8,128)(2,1)} %all-gather.9.cloned.1.call-done, bf16[1024,2048]{1,0:T(8,128)(2,1)S(1)} %get-tuple-element.27, f32[2048]{0:T(1024)S(1)} %copy-done.17, f32[1024]{0:T(1024)S(1)} %add_rsqrt_fusion.1), kind=kOutput, calls=%fused_computation.33 | convolution fusion | flops 3229614080 | bytes 10498048 | tf_op jit(solution)/shard_map/dot_general | solution.py:187
  326.2 14.1 %fusion.23 = f32[1024,2048]{1,0:T(8,128)} fusion(bf16[768,2048]{1,0:T(8,128)(2,1)} %all-gather.13.cloned.1.call-done, f32[1024,768]{1,0:T(8,128)} %fusion.20, bf16[2048,768]{0,1:T(8,128)(2,1)} %all-gather.11.cloned.1.call-done, bf16[1024,2048]{1,0:T(8,128)(2,1)} %copy-done.7, f32[2048]{0:T(1024)S(1)} %copy-done.17, f32[1024]{0:T(1024)S(1)} %add_rsqrt_fusion.1), kind=kOutput, calls=%fused_computation.34 | convolution fusion | flops 6455558144 | bytes 22032384 | tf_op jit(solution)/shard_map/dot_general | solution.py:190
  340.2 1.6 slice.65
  342.6 56.0 %all-reduce.2.cloned.1.call-done = f32[9,2048]{1,0:T(8,128)} async-done(((f32[9,2048]{1,0:T(8,128)}), f32[9,2048]{1,0:T(8,128)}) %all-reduce.2.cloned.1.call-update) | async-done | bytes 73744 | tf_op jit(solution)/shard_map/psum | solution.py:197
  400.6 53.5 %reduce-scatter.2.cloned.1.call-done = f32[128,2048]{1,0:T(8,128)} async-done(((f32[1024,2048]{1,0:T(8,128)}), f32[128,2048]{1,0:T(8,128)}) %reduce-scatter.2.cloned.1.call-update) | async-done | bytes 1048592 | tf_op jit(solution)/shard_map/reduce_scatter | solution.py:191
  454.1 2.6 scatter_custom_fusion
  458.9 8.4 %all-to-all-start.1 = ((bf16[128,2,1024]{2,1,0:T(2,128)(2,1)}), bf16[128,2,1024]{2,1,0:T(2,128)(2,1)S(1)}, u32[]{:S(2)}, u32[]{:S(2)}) async-start(bf16[128,2,1024]{2,1,0:T(2,128)(2,1)} %reshape.452), calls=%async_computation.2 | async-start | bytes 1048576 | tf_op jit(solution)/shard_map/all_to_all | solution.py:77
  467.3 22.4 %all-gather.1 = bf16[16,9,2048]{2,1,0:T(8,128)(2,1)S(1)} all-gather(bf16[1,9,2048]{2,1,0:T(8,128)(2,1)S(1)} %fusion.51), channel_id=1, replica_groups=mesh['req'=16,'kv'=8] {'req'}, dimensions={0}, use_global_device_ids=true | all-gather | bytes 626688 | tf_op jit(solution)/shard_map/all_gather | solution.py:202
  490.8 4.4 convolution_reduce_fusion
  495.2 68.5 %pmax.7 = f32[144]{0:T(256)} all-reduce(f32[144]{0:T(256)S(1)} %convolution_reduce_fusion), channel_id=1, replica_groups=mesh['req'=16,'kv'=8] {'req','kv'}, use_global_device_ids=true, to_apply=%region_15.16 | all-reduce | flops 144 | bytes 1152 | tf_op jit(solution)/shard_map/pmax | solution.py:208
  564.2 2.4 scatter_custom_fusion.1
  (106 shorter events, 25.7 us)
Async XLA Ops:
  7.2 34.2 %copy-start = (bf16[2048,384]{1,0:T(8,128)(2,1)S(1)}, bf16[2048,384]{1,0:T(8,128)(2,1)}, u32[]{:S(2)}) copy-start(bf16[2048,384]{1,0:T(8,128)(2,1)} %param.37) | copy-start | bytes 4718596
  13.5 25.2 %all-to-all-start = ((bf16[128,2,1024]{2,1,0:T(2,128)(2,1)}), bf16[128,2,1024]{2,1,0:T(2,128)(2,1)S(1)}, u32[]{:S(2)}, u32[]{:S(2)}) async-start(bf16[128,2,1024]{2,1,0:T(2,128)(2,1)} %reshape.450), calls=%async_computation | async-start | bytes 1048576 | tf_op jit(solution)/shard_map/all_to_all | solution.py:77
  25.0 45.1 %all-gather.19.cloned.1.call-start = ((), (), s32[]{:S(2)}) async-start(), calls=%async_computation.10 | async-start | bytes 4718592 | tf_op jit(solution)/shard_map/all_gather | solution.py:115
  41.2 7.1 %copy-start.10 = (s32[8]{0:T(128)S(1)}, s32[8]{0:T(128)}, u32[]{:S(2)}) copy-start(s32[8]{0:T(128)} %param.23) | copy-start | bytes 100
  41.3 79.3 %all-gather.9.cloned.1.call-start = ((), (), s32[]{:S(2)}) async-start(), calls=%async_computation.3 | async-start | bytes 3342336 | tf_op jit(solution)/shard_map/all_gather | solution.py:120
  42.5 126.3 %all-gather.11.cloned.1.call-start = ((), (), s32[]{:S(2)}) async-start(), calls=%async_computation.4 | async-start | bytes 3342336 | tf_op jit(solution)/shard_map/all_gather | solution.py:126
  44.8 172.8 %all-gather.13.cloned.1.call-start = ((), (), s32[]{:S(2)}) async-start(), calls=%async_computation.5 | async-start | bytes 3342336 | tf_op jit(solution)/shard_map/all_gather | solution.py:132
  46.5 221.9 %all-gather.17.cloned.1.call-start = ((), (), s32[]{:S(2)}) async-start(), calls=%async_computation.7 | async-start | bytes 9437184 | tf_op jit(solution)/shard_map/all_gather | solution.py:117
  47.1 255.8 %all-gather.15.cloned.1.call-start = ((), (), s32[]{:S(2)}) async-start(), calls=%async_computation.6 | async-start | bytes 4718592 | tf_op jit(solution)/shard_map/all_gather | solution.py:182
  48.5 24.9 %copy-start.8 = (f32[2048]{0:T(1024)S(1)}, f32[2048]{0:T(1024)}, u32[]{:S(2)}) copy-start(f32[2048]{0:T(1024)} %param.29) | copy-start | bytes 24580
  70.1 3.4 copy-start.2
  73.6 1.2 copy-start.13
  74.8 2.3 copy-start.3
  74.8 3.9 copy-start.6
  77.1 5.3 copy-start.11
  78.7 5.4 copy-start.12
  84.1 2.2 copy-start.4
  84.9 3.2 copy-start.14
  88.1 3.7 copy-start.5
  88.2 4.5 copy-start.15
  92.6 15.9 %copy-start.16 = (bf16[1,2048,128]{2,1,0:T(8,128)(2,1)S(1)}, bf16[1,2048,128]{2,1,0:T(8,128)(2,1)}, u32[]{:S(2)}) copy-start(bf16[1,2048,128]{2,1,0:T(8,128)(2,1)} %param.28) | copy-start | bytes 1572868
  218.7 100.3 %copy-start.17 = (f32[2048]{0:T(1024)S(1)}, f32[2048]{0:T(1024)}, u32[]{:S(2)}) copy-start(f32[2048]{0:T(1024)} %param.36) | copy-start | bytes 24580
  218.7 179.8 %all-reduce.2.cloned.1.call-start = ((), (), s32[]{:S(2)}) async-start(), calls=%async_computation.9 | async-start | bytes 262144 | tf_op jit(solution)/shard_map/psum | solution.py:197
  317.1 1.9 copy-start.7
  341.8 57.8 %copy-start.9 = (f32[2048]{0:T(1024)S(1)}, f32[2048]{0:T(1024)}, u32[]{:S(2)}) copy-start(f32[2048]{0:T(1024)} %param.40) | copy-start | bytes 24580
  341.8 112.3 %reduce-scatter.2.cloned.1.call-start = ((), (), s32[]{:S(2)}) async-start(), calls=%async_computation.8 | async-start | bytes 9437184 | tf_op jit(solution)/shard_map/reduce_scatter | solution.py:191
  458.9 104.8 %all-to-all-start.1 = ((bf16[128,2,1024]{2,1,0:T(2,128)(2,1)}), bf16[128,2,1024]{2,1,0:T(2,128)(2,1)S(1)}, u32[]{:S(2)}, u32[]{:S(2)}) async-start(bf16[128,2,1024]{2,1,0:T(2,128)(2,1)} %reshape.452), calls=%async_computation.2 | async-start | bytes 1048576 | tf_op jit(solution)/shard_map/all_to_all | solution.py:77
  489.7 76.9 %copy-start.1 = (bf16[2048,384]{1,0:T(8,128)(2,1)S(1)}, bf16[2048,384]{1,0:T(8,128)(2,1)}, u32[]{:S(2)}) copy-start(bf16[2048,384]{1,0:T(8,128)(2,1)} %param.37) | copy-start | bytes 4718596
Sparse Core Ops, SparseCore 0:
  41.4 28.7 all-gather.18
  72.3 47.3 all-gather.8
  121.8 46.8 all-gather.10
  170.8 46.8 all-gather.12
  219.2 49.1 all-gather.16
  270.6 32.2 all-gather.14
  341.9 56.5 all-reduce.1
  401.1 52.9 reduce-scatter.1
where the time goes:
time: 578 us; the launch traced here: 574 us
  waiting for transfers between devices  321 us (56%)
  blocking collectives  90.9 us (16%)
  matrix products  79.3 us (14%)
  local copies, waits for them, and re-layouts  24.9 us (4%)
  other arithmetic  21.6 us (4%)
  starting transfers between devices  20.8 us (4%)
  between operations  15.5 us (3%)
    pmax x1, blocking collectives, shards(): max_logit = lax.pmax(local_peaks, ('req', 'kv'))  68.5 us
    psum x1, waiting for transfers between devices, shards(): tail_sum = lax.psum(down_part[fresh_count - 1:], 'kv')  56 us
    reduce_scatter x1, waiting for transfers between devices, shards(): lax.psum_scatter(down_part, 'kv', scatter_dimension=0, tiled=True)  53.5 us
    all_gather x1, waiting for transfers between devices, shards(): o_full = lax.all_gather(o_proj, 'kv', axis=0, tiled=True)  49.7 us
    all_gather x1, waiting for transfers between devices, shards(): lax.all_gather(lax.dynamic_slice_in_dim(w_down, kv_index * ff_piece, ff_p...  48.9 us
    all_gather x1, waiting for transfers between devices, shards(): lax.all_gather(lax.dynamic_slice_in_dim(w_up, kv_index * ff_piece, ff_pie...  48.2 us
    all_gather x1, waiting for transfers between devices, shards(): lax.all_gather(pieces.reshape(tok_req, q_cols), 'kv', axis=1, tiled=True)  34.4 us
    all_gather x1, blocking collectives, shards(): lax.all_gather(tail_rows, 'req', axis=0, tiled=True)  22.4 us
  transfers between devices with their start and end apart: 10, of which 8 were waited for; matrix products, arithmetic and copies ran while one was open for 12% of the time, Pallas kernels for 0%

commit v1 on v0

--- a/solution.py
+++ b/solution.py
@@ -112,7 +112,20 @@
     slot_place = lax.dynamic_index_in_dim(slot_table, self_index, 0, keepdims=False) // rows_dev
     arrived = regroup(hidden_in[send_rows])
     owner_rows = arrived[slot_place]
-    rows_all = lax.all_gather(owner_rows, "kv", axis=0, tiled=True)
+    found = []
+    n_lanes = jax.lax.psum(1, "kv")
+    for j in range(1, n_lanes):
+        found.append((j - 1, j))
+    oldest = found + [(n_lanes - 1, 0)]
+    part_now = owner_rows
+    vals = [part_now]
+    for _ in range(n_lanes - 1):
+        part_now = jax.lax.ppermute(part_now, "kv", oldest)
+        vals += [part_now]
+    current_value = jnp.concatenate([*reversed(vals)], 0)
+    rows_all = jnp.roll(
+        current_value, shift=(jax.lax.axis_index("kv") + 1) * part_now.shape[0], axis=0
+    )
     normed = norm_rows(rows_all, attn_gain).astype(jnp.bfloat16)
     o_full = lax.all_gather(o_proj, "kv", axis=0, tiled=True)
     ff_dev = w_gate.shape[1]

time: 578 us -> 529 us (0.915)
  waiting for transfers between devices: 321 us -> 246 us
  starting transfers between devices: 20.8 us -> 35 us
  local copies, waits for them, and re-layouts: 24.9 us -> 30.7 us
    all_gather x1, waiting for transfers between devices: 48.9 us -> 0.02 us  [shards(): lax.all_gather(lax.dynamic_slice_in_dim(w_down, kv_index * ff_piece, ff_p...]
    all_gather x1, waiting for transfers between devices: 48.2 us -> 0.02 us  [shards(): lax.all_gather(lax.dynamic_slice_in_dim(w_up, kv_index * ff_piece, ff_pie...]
    ppermute x0 -> x7, waiting for transfers between devices: none -> 36.7 us  [shards(): part_now = jax.lax.ppermute(part_now, 'kv', oldest)]
    all_gather x1 -> x0, waiting for transfers between devices: 15.7 us -> none  [shards(): rows_all = lax.all_gather(owner_rows, 'kv', axis=0, tiled=True)]
    ppermute x0 -> x7, starting transfers between devices: none -> 14.8 us  [shards(): part_now = jax.lax.ppermute(part_now, 'kv', oldest)]
    unnamed x44 -> x57, local copies, waits for them, and re-layouts: 9.87 us -> 16.4 us
  transfers between devices with their start and end apart: 10 -> 16, of which waited for: 8 -> 12; matrix products, arithmetic and copies ran while one was open for 12% -> 16% of each run, Pallas kernels for 0% -> 0%
where the time goes in v1:
time: 529 us; the launch traced here: 523 us
  waiting for transfers between devices  246 us (47%)
  blocking collectives  90.9 us (17%)
  matrix products  84 us (16%)
  starting transfers between devices  35 us (7%)
  local copies, waits for them, and re-layouts  30.7 us (6%)
  other arithmetic  20.8 us (4%)
  between operations  15.6 us (3%)
    pmax x1, blocking collectives, shards(): max_logit = lax.pmax(local_peaks, ('req', 'kv'))  68.6 us
    psum x1, waiting for transfers between devices, shards(): tail_sum = lax.psum(down_part[fresh_count - 1:], 'kv')  56.3 us
    reduce_scatter x1, waiting for transfers between devices, shards(): lax.psum_scatter(down_part, 'kv', scatter_dimension=0, tiled=True)  53.4 us
    all_gather x1, waiting for transfers between devices, shards(): o_full = lax.all_gather(o_proj, 'kv', axis=0, tiled=True)  51.3 us
    ppermute x7, waiting for transfers between devices, shards(): part_now = jax.lax.ppermute(part_now, 'kv', oldest)  36.7 us
    all_gather x1, waiting for transfers between devices, shards(): lax.all_gather(pieces.reshape(tok_req, q_cols), 'kv', axis=1, tiled=True)  34 us
    all_gather x1, blocking collectives, shards(): lax.all_gather(tail_rows, 'req', axis=0, tiled=True)  22.4 us
    all_to_all x2, starting transfers between devices, regroup(): lax.all_to_all(rows_in, ('req', 'kv'), split_axis=0, concat_axis=0, tiled...  19.9 us
  transfers between devices with their start and end apart: 16, of which 12 were waited for; matrix products, arithmetic and copies ran while one was open for 16% of the time, Pallas kernels for 0%

profile of v1, /device:TPU:1, one launch (start us, length us, event | category | flops | bytes accessed | tf_op | source)
XLA Modules:
  0.0 523.0 jit_solution(8011846986419430282)
XLA Ops:
  13.1 2.6 gather_fusion
  18.3 11.5 %all-to-all-start = ((bf16[128,2,1024]{2,1,0:T(2,128)(2,1)}), bf16[128,2,1024]{2,1,0:T(2,128)(2,1)S(1)}, u32[]{:S(2)}, u32[]{:S(2)}) async-start(bf16[128,2,1024]{2,1,0:T(2,128)(2,1)} %reshape.449), calls=%async_computation | async-start | bytes 1048576 | tf_op jit(solution)/shard_map/all_to_all | solution.py:77
  30.6 13.0 %all-to-all-done = bf16[128,2,1024]{2,1,0:T(2,128)(2,1)S(1)} async-done(((bf16[128,2,1024]{2,1,0:T(2,128)(2,1)}), bf16[128,2,1024]{2,1,0:T(2,128)(2,1)S(1)}, u32[]{:S(2)}, u32[]{:S(2)}) %all-to-all-start) | async-done | bytes 524320 | tf_op jit(solution)/shard_map/all_to_all | solution.py:77
  46.3 6.1 %collective-permute-done = bf16[128,2048]{1,0:T(8,128)(2,1)S(1)} collective-permute-done((bf16[128,2048]{1,0:T(8,128)(2,1)S(1)}, bf16[128,2048]{1,0:T(8,128)(2,1)S(1)}, u32[]{:S(2)}, u32[]{:S(2)}) %collective-permute-start) | collective-permute-done | bytes 524320 | tf_op jit(solution)/shard_map/ppermute | solution.py:123
  52.4 2.5 collective-permute-start.1
  54.9 6.1 %collective-permute-done.1 = bf16[128,2048]{1,0:T(8,128)(2,1)S(1)} collective-permute-done((bf16[128,2048]{1,0:T(8,128)(2,1)S(1)}, bf16[128,2048]{1,0:T(8,128)(2,1)S(1)}, u32[]{:S(2)}, u32[]{:S(2)}) %collective-permute-start.1) | collective-permute-done | bytes 524320 | tf_op jit(solution)/shard_map/ppermute | solution.py:123
  61.1 2.5 collective-permute-start.2
  63.5 6.1 %collective-permute-done.2 = bf16[128,2048]{1,0:T(8,128)(2,1)S(1)} collective-permute-done((bf16[128,2048]{1,0:T(8,128)(2,1)S(1)}, bf16[128,2048]{1,0:T(8,128)(2,1)S(1)}, u32[]{:S(2)}, u32[]{:S(2)}) %collective-permute-start.2) | collective-permute-done | bytes 524320 | tf_op jit(solution)/shard_map/ppermute | solution.py:123
  74.5 3.8 collective-permute-done.3
  80.9 6.0 %collective-permute-done.4 = bf16[128,2048]{1,0:T(8,128)(2,1)S(1)} collective-permute-done((bf16[128,2048]{1,0:T(8,128)(2,1)S(1)}, bf16[128,2048]{1,0:T(8,128)(2,1)S(1)}, u32[]{:S(2)}, u32[]{:S(2)}) %collective-permute-start.4) | collective-permute-done | bytes 524320 | tf_op jit(solution)/shard_map/ppermute | solution.py:123
  89.4 4.0 fusion.4
  93.4 3.4 collective-permute-done.5
  98.1 3.6 multiply_cosine_fusion
  101.7 5.2 collective-permute-done.6
  119.7 3.7 multiply_reduce_fusion.1
  126.0 3.6 fusion.77
  130.2 3.6 convolution_convert_fusion
  133.8 2.9 fusion.48
  136.8 16.0 %fusion.78 = (f32[2,1016]{1,0:T(2,128)S(1)}, f32[2,1016,3064]{2,1,0:T(8,128)}) fusion(pred[1016,3064]{1,0:T(8,128)(4,1)} %fusion.4, bf16[1016,128]{1,0:T(8,128)(2,1)S(1)} %copy.47, bf16[2048,128]{1,0:T(8,128)(2,1)S(1)} %bitcast.93, bf16[1024,2,64]{2,0,1:T(8,128)(2,1)S(1)} %get-tuple-element.10, bf16[1024,2,64]{2,0,1:T(8,128)(2,1)S(1)} %get-tuple-element.11), kind=kOutput, calls=%fused_computation.160 | convolution fusion | flops 1621384704 | bytes 29334016 | tf_op jit(solution)/shard_map/sub | solution.py:48
  152.8 12.0 %fusion.18 = bf16[1016,2,128]{2,0,1:T(8,128)(2,1)S(1)} fusion(f32[2,1016,3064]{2,1,0:T(8,128)} %get-tuple-element.25, f32[2,1016]{1,0:T(2,128)S(1)} %get-tuple-element.24, bf16[1016,128]{1,0:T(8,128)(2,1)S(1)} %slice.54, bf16[2048,128]{1,0:T(8,128)(2,1)S(1)} %bitcast.94), kind=kOutput, calls=%fused_computation.32 | convolution fusion | flops 1608149248 | bytes 26216896 | tf_op jit(solution)/shard_map/gck,kd->cgd/dot_general | solution.py:50
  166.6 34.0 %all-gather.13.cloned.1.call-done = bf16[1024,2048]{0,1:T(8,128)(2,1)} async-done(((bf16[1024,256]{0,1:T(8,128)(2,1)}), bf16[1024,2048]{0,1:T(8,128)(2,1)}) %all-gather.13.cloned.1.call-update) | async-done | bytes 4194320 | tf_op jit(solution)/shard_map/all_gather | solution.py:195
  200.6 51.3 %all-gather.15.cloned.1.call-done = bf16[2048,2048]{1,0:T(8,128)(2,1)} async-done(((bf16[256,2048]{1,0:T(8,128)(2,1)}), bf16[2048,2048]{1,0:T(8,128)(2,1)}) %all-gather.15.cloned.1.call-update) | async-done | bytes 8388624 | tf_op jit(solution)/shard_map/all_gather | solution.py:130
  251.9 14.2 %fusion.7 = (f32[1024]{0:T(1024)S(1)}, bf16[1024,2048]{1,0:T(8,128)(2,1)S(1)}) fusion(bf16[1024,2048]{0,1:T(8,128)(2,1)} %all-gather.13.cloned.1.call-done, bf16[2048,2048]{1,0:T(8,128)(2,1)} %all-gather.15.cloned.1.call-done, bf16[2048,2048]{1,0:T(8,128)(2,1)} %copy-done.3, s32[]{:T(128)S(6)} %select_n.91), kind=kOutput, calls=%fused_computation.20 | convolution fusion | flops 8602516480 | bytes 20975620 | tf_op jit(solution)/shard_map/dot_general | solution.py:197
  268.0 7.1 %fusion.20 = f32[1024,768]{1,0:T(8,128)} fusion(bf16[2048,768]{0,1:T(8,128)(2,1)} %all-gather.7.cloned.1.call-done, bf16[1024,2048]{1,0:T(8,128)(2,1)S(1)} %get-tuple-element.27, f32[2048]{0:T(1024)S(1)} %copy-done.16, f32[1024]{0:T(1024)S(1)} %add_rsqrt_fusion.1), kind=kOutput, calls=%fused_computation.33 | convolution fusion | flops 3229614080 | bytes 10498048 | tf_op jit(solution)/shard_map/dot_general | solution.py:200
  275.2 14.1 %fusion.23 = f32[1024,2048]{1,0:T(8,128)} fusion(bf16[768,2048]{1,0:T(8,128)(2,1)} %all-gather.11.cloned.1.call-done, f32[1024,768]{1,0:T(8,128)} %fusion.20, bf16[2048,768]{0,1:T(8,128)(2,1)} %all-gather.9.cloned.1.call-done, bf16[1024,2048]{1,0:T(8,128)(2,1)} %copy-done.7, f32[2048]{0:T(1024)S(1)} %copy-done.16, f32[1024]{0:T(1024)S(1)} %add_rsqrt_fusion.1), kind=kOutput, calls=%fused_computation.34 | convolution fusion | flops 6455558144 | bytes 22032384 | tf_op jit(solution)/shard_map/dot_general | solution.py:203
  291.6 56.3 %all-reduce.2.cloned.1.call-done = f32[9,2048]{1,0:T(8,128)} async-done(((f32[9,2048]{1,0:T(8,128)}), f32[9,2048]{1,0:T(8,128)}) %all-reduce.2.cloned.1.call-update) | async-done | bytes 73744 | tf_op jit(solution)/shard_map/psum | solution.py:210
  350.0 53.4 %reduce-scatter.2.cloned.1.call-done = f32[128,2048]{1,0:T(8,128)} async-done(((f32[1024,2048]{1,0:T(8,128)}), f32[128,2048]{1,0:T(8,128)}) %reduce-scatter.2.cloned.1.call-update) | async-done | bytes 1048592 | tf_op jit(solution)/shard_map/reduce_scatter | solution.py:204
  403.4 2.6 scatter_custom_fusion
  408.2 8.4 %all-to-all-start.1 = ((bf16[128,2,1024]{2,1,0:T(2,128)(2,1)}), bf16[128,2,1024]{2,1,0:T(2,128)(2,1)S(1)}, u32[]{:S(2)}, u32[]{:S(2)}) async-start(bf16[128,2,1024]{2,1,0:T(2,128)(2,1)} %reshape.451), calls=%async_computation.2 | async-start | bytes 1048576 | tf_op jit(solution)/shard_map/all_to_all | solution.py:77
  416.6 22.4 %all-gather = bf16[16,9,2048]{2,1,0:T(8,128)(2,1)S(1)} all-gather(bf16[1,9,2048]{2,1,0:T(8,128)(2,1)S(1)} %fusion.51), channel_id=1, replica_groups=mesh['req'=16,'kv'=8] {'req'}, dimensions={0}, use_global_device_ids=true | all-gather | bytes 626688 | tf_op jit(solution)/shard_map/all_gather | solution.py:215
  440.1 4.4 convolution_reduce_fusion
  444.4 68.6 %pmax.7 = f32[144]{0:T(256)} all-reduce(f32[144]{0:T(256)S(1)} %convolution_reduce_fusion), channel_id=1, replica_groups=mesh['req'=16,'kv'=8] {'req','kv'}, use_global_device_ids=true, to_apply=%region_15.16 | all-reduce | flops 144 | bytes 1152 | tf_op jit(solution)/shard_map/pmax | solution.py:221
  (131 shorter events, 52.7 us)
Async XLA Ops:
  7.2 157.7 %all-gather.7.cloned.1.call-start = ((), (), s32[]{:S(2)}) async-start(), calls=%async_computation.3 | async-start | bytes 3342336 | tf_op jit(solution)/shard_map/all_gather | solution.py:133
  9.7 155.2 %all-gather.9.cloned.1.call-start = ((), (), s32[]{:S(2)}) async-start(), calls=%async_computation.4 | async-start | bytes 3342336 | tf_op jit(solution)/shard_map/all_gather | solution.py:139
  12.1 68.7 %copy-start.10 = (s32[8]{0:T(128)S(1)}, s32[8]{0:T(128)}, u32[]{:S(2)}) copy-start(s32[8]{0:T(128)} %param.23) | copy-start | bytes 100
  18.3 25.2 %all-to-all-start = ((bf16[128,2,1024]{2,1,0:T(2,128)(2,1)}), bf16[128,2,1024]{2,1,0:T(2,128)(2,1)S(1)}, u32[]{:S(2)}, u32[]{:S(2)}) async-start(bf16[128,2,1024]{2,1,0:T(2,128)(2,1)} %reshape.449), calls=%async_computation | async-start | bytes 1048576 | tf_op jit(solution)/shard_map/all_to_all | solution.py:77
  29.8 135.1 %all-gather.11.cloned.1.call-start = ((), (), s32[]{:S(2)}) async-start(), calls=%async_computation.5 | async-start | bytes 3342336 | tf_op jit(solution)/shard_map/all_gather | solution.py:145
  45.3 7.2 %collective-permute-start = (bf16[128,2048]{1,0:T(8,128)(2,1)S(1)}, bf16[128,2048]{1,0:T(8,128)(2,1)S(1)}, u32[]{:S(2)}, u32[]{:S(2)}) collective-permute-start(bf16[128,2048]{1,0:T(8,128)(2,1)S(1)} %gather_fusion.1), channel_id=1, source_target_pairs={{0,1},{1,2},{2,3},{3,4},{4,5},{5,6},{6,7},{7,0},{8,9},{9,10},{10,1... | collective-permute-start | bytes 1572872 | tf_op jit(solution)/shard_map/ppermute | solution.py:123
  52.4 8.6 %collective-permute-start.1 = (bf16[128,2048]{1,0:T(8,128)(2,1)S(1)}, bf16[128,2048]{1,0:T(8,128)(2,1)S(1)}, u32[]{:S(2)}, u32[]{:S(2)}) collective-permute-start(bf16[128,2048]{1,0:T(8,128)(2,1)S(1)} %collective-permute-done), channel_id=1, source_target_pairs={{0,1},{1,2},{2,3},{3,4},{4,5},{5,6},{6,7},{7,0},{8,9},{9,10},{10,1... | collective-permute-start | bytes 1572872 | tf_op jit(solution)/shard_map/ppermute | solution.py:123
  61.1 8.6 %collective-permute-start.2 = (bf16[128,2048]{1,0:T(8,128)(2,1)S(1)}, bf16[128,2048]{1,0:T(8,128)(2,1)S(1)}, u32[]{:S(2)}, u32[]{:S(2)}) collective-permute-start(bf16[128,2048]{1,0:T(8,128)(2,1)S(1)} %collective-permute-done.1), channel_id=1, source_target_pairs={{0,1},{1,2},{2,3},{3,4},{4,5},{5,6},{6,7},{7,0},{8,9},{9,10},{10,1... | collective-permute-start | bytes 1572872 | tf_op jit(solution)/shard_map/ppermute | solution.py:123
  69.7 8.6 %collective-permute-start.3 = (bf16[128,2048]{1,0:T(8,128)(2,1)S(1)}, bf16[128,2048]{1,0:T(8,128)(2,1)S(1)}, u32[]{:S(2)}, u32[]{:S(2)}) collective-permute-start(bf16[128,2048]{1,0:T(8,128)(2,1)S(1)} %collective-permute-done.2), channel_id=1, source_target_pairs={{0,1},{1,2},{2,3},{3,4},{4,5},{5,6},{6,7},{7,0},{8,9},{9,10},{10,1... | collective-permute-start | bytes 1572872 | tf_op jit(solution)/shard_map/ppermute | solution.py:123
  73.8 126.9 %all-gather.13.cloned.1.call-start = ((), (), s32[]{:S(2)}) async-start(), calls=%async_computation.6 | async-start | bytes 4718592 | tf_op jit(solution)/shard_map/all_gather | solution.py:195
  78.3 8.6 %collective-permute-start.4 = (bf16[128,2048]{1,0:T(8,128)(2,1)S(1)}, bf16[128,2048]{1,0:T(8,128)(2,1)S(1)}, u32[]{:S(2)}, u32[]{:S(2)}) collective-permute-start(bf16[128,2048]{1,0:T(8,128)(2,1)S(1)} %collective-permute-done.3), channel_id=1, source_target_pairs={{0,1},{1,2},{2,3},{3,4},{4,5},{5,6},{6,7},{7,0},{8,9},{9,10},{10,1... | collective-permute-start | bytes 1572872 | tf_op jit(solution)/shard_map/ppermute | solution.py:123
  86.9 9.9 %collective-permute-start.5 = (bf16[128,2048]{1,0:T(8,128)(2,1)S(1)}, bf16[128,2048]{1,0:T(8,128)(2,1)}, u32[]{:S(2)}, u32[]{:S(2)}) collective-permute-start(bf16[128,2048]{1,0:T(8,128)(2,1)S(1)} %collective-permute-done.4), channel_id=1, source_target_pairs={{0,1},{1,2},{2,3},{3,4},{4,5},{5,6},{6,7},{7,0},{8,9},{9,10},{10,1... | collective-permute-start | bytes 1572872 | tf_op jit(solution)/shard_map/ppermute | solution.py:123
  96.8 10.1 %collective-permute-start.6 = (bf16[128,2048]{1,0:T(8,128)(2,1)}, bf16[128,2048]{1,0:T(8,128)(2,1)}, u32[]{:S(2)}, u32[]{:S(2)}) collective-permute-start(bf16[128,2048]{1,0:T(8,128)(2,1)} %collective-permute-done.5), channel_id=1, source_target_pairs={{0,1},{1,2},{2,3},{3,4},{4,5},{5,6},{6,7},{7,0},{8,9},{9,10},{10,1... | collective-permute-start | bytes 1572872 | tf_op jit(solution)/shard_map/ppermute | solution.py:123
  109.2 3.6 copy-start.8
  111.6 4.1 copy-start.13
  111.8 6.2 %copy-start.3 = (bf16[2048,2048]{1,0:T(8,128)(2,1)}, bf16[2048,2048]{1,0:T(8,128)(2,1)S(1)}, u32[]{:S(2)}) copy-start(bf16[2048,2048]{1,0:T(8,128)(2,1)S(1)} %constant_dynamic-update-slice_fusion) | copy-start | bytes 25165828
  113.8 1.9 copy-start.2
  115.7 4.0 copy-start.6
  115.7 7.7 %copy-start.11 = (f32[128]{0:T(128)S(1)}, f32[128]{0:T(128)}, u32[]{:S(2)}) copy-start(f32[128]{0:T(128)} %param.34) | copy-start | bytes 1540
  115.7 9.2 %copy-start.12 = (f32[128]{0:T(128)S(1)}, f32[128]{0:T(128)}, u32[]{:S(2)}) copy-start(f32[128]{0:T(128)} %param.33) | copy-start | bytes 1540
  118.1 7.2 %copy-start.4 = (f32[1024,64]{1,0:T(8,128)S(1)}, f32[1024,64]{1,0:T(8,128)}, u32[]{:S(2)}) copy-start(f32[1024,64]{1,0:T(8,128)} %get-tuple-element.16) | copy-start | bytes 786436
  118.1 7.2 %copy-start.5 = (f32[1024,64]{1,0:T(8,128)S(1)}, f32[1024,64]{1,0:T(8,128)}, u32[]{:S(2)}) copy-start(f32[1024,64]{1,0:T(8,128)} %get-tuple-element.17) | copy-start | bytes 786436
  126.0 10.9 %copy-start.14 = (bf16[1,2048,128]{2,1,0:T(8,128)(2,1)S(1)}, bf16[1,2048,128]{2,1,0:T(8,128)(2,1)}, u32[]{:S(2)}) copy-start(bf16[1,2048,128]{2,1,0:T(8,128)(2,1)} %param.27) | copy-start | bytes 1572868
  136.8 16.0 %copy-start.15 = (bf16[1,2048,128]{2,1,0:T(8,128)(2,1)S(1)}, bf16[1,2048,128]{2,1,0:T(8,128)(2,1)}, u32[]{:S(2)}) copy-start(bf16[1,2048,128]{2,1,0:T(8,128)(2,1)} %param.28) | copy-start | bytes 1572868
  166.0 85.9 %all-gather.15.cloned.1.call-start = ((), (), s32[]{:S(2)}) async-start(), calls=%async_computation.7 | async-start | bytes 9437184 | tf_op jit(solution)/shard_map/all_gather | solution.py:130
  166.5 101.5 %copy-start.16 = (f32[2048]{0:T(1024)S(1)}, f32[2048]{0:T(1024)}, u32[]{:S(2)}) copy-start(f32[2048]{0:T(1024)} %param.36) | copy-start | bytes 24580
  166.6 181.3 %all-reduce.2.cloned.1.call-start = ((), (), s32[]{:S(2)}) async-start(), calls=%async_computation.9 | async-start | bytes 262144 | tf_op jit(solution)/shard_map/psum | solution.py:210
  266.1 2.0 copy-start.7
  289.2 59.7 %copy-start.9 = (f32[2048]{0:T(1024)S(1)}, f32[2048]{0:T(1024)}, u32[]{:S(2)}) copy-start(f32[2048]{0:T(1024)} %param.40) | copy-start | bytes 24580
  290.8 112.6 %reduce-scatter.2.cloned.1.call-start = ((), (), s32[]{:S(2)}) async-start(), calls=%async_computation.8 | async-start | bytes 9437184 | tf_op jit(solution)/shard_map/reduce_scatter | solution.py:204
  348.9 167.0 %copy-start.1 = (bf16[2048,384]{1,0:T(8,128)(2,1)S(1)}, bf16[2048,384]{1,0:T(8,128)(2,1)}, u32[]{:S(2)}) copy-start(bf16[2048,384]{1,0:T(8,128)(2,1)} %param.37) | copy-start | bytes 4718596
  408.2 104.8 %all-to-all-start.1 = ((bf16[128,2,1024]{2,1,0:T(2,128)(2,1)}), bf16[128,2,1024]{2,1,0:T(2,128)(2,1)S(1)}, u32[]{:S(2)}, u32[]{:S(2)}) async-start(bf16[128,2,1024]{2,1,0:T(2,128)(2,1)} %reshape.451), calls=%async_computation.2 | async-start | bytes 1048576 | tf_op jit(solution)/shard_map/all_to_all | solution.py:77
  (1 other events, 1.4 us)
Sparse Core Ops, SparseCore 0:
  10.2 55.7 all-gather.6
  68.0 46.8 all-gather.8
  117.1 46.9 all-gather.10
  166.2 34.3 all-gather.12
  202.2 49.6 all-gather.14
  291.0 56.8 all-reduce.1
  350.4 52.9 reduce-scatter.1
